TPU v7x, 128 devices: a whole 4x4x4 slice. The times are simulated.
128 devices in a mesh: ctx: 32 (over z, x, y_lo), tp: 4 (over y_hi, core).
Axes of the slice: x: 4, y: 4 (y_hi: 2, y_lo: 2; y = y_hi * 2 + y_lo), z: 4, core: 2. Of those that a mesh axis runs over, the one named last changes fastest.
Arguments:
- signal: bfloat16 [4096, 2048], P('ctx', 'tp'), may hold values from -6 to 6
- gate: bfloat16 [4096, 2048], P('ctx', 'tp'), may hold values from -6 to 6
- filt: bfloat16 [4096, 2048], P('ctx', 'tp'), may hold values from -0.25 to 0.25
- bias: float32 [2048], P('tp'), may hold values from -2 to 2
- doc_ids: int32 [4096], replicated, may hold values from 0 to 3, never falling along the last dimension, each value on 1 to 3840 neighbouring positions
- block_perm: int32 [64], replicated, may hold values from 0 to 63, each once
- out_weight: bfloat16 [2048, 2048], P('tp'), may hold values from -0.125 to 0.125
Outputs:
- mixed: bfloat16 [4096, 2048], P('ctx', 'tp')
Inputs may be any that keep to these rules, and one draw needn't show every extreme that they name: `doc_ids`: ids never fall along the sequence; each document is a run of 1 to 3840 positions, one exactly 3840. `block_perm`: each block number once.
All inputs are finite; a program needn't handle non-finite values.
Results may differ from a plain program's by a relative error of at most 0.012.
Values may be sent and summed in bfloat16 or wider, within the bound.
No kernel may reach another device: no remote copies, remote signals or barrier semaphores. Data moves between devices by JAX's collectives and lax.ppermute only.
A program may use at most 64 MiB of HBM per device.

v0:
```python
import math
import jax
import jax.numpy as jnp
from jax import lax
from jax.sharding import PartitionSpec as P

SPAN = 64


def split_table(table):
    upper_part = table.astype(jnp.bfloat16)
    lower_part = (table - upper_part.astype(jnp.float32)).astype(jnp.bfloat16)
    return (upper_part, lower_part)


def transform_many(divide_pair_table, input_values):
    first_position = jnp.einsum(
        "ol,wld->wod", divide_pair_table[0], input_values, preferred_element_type=jnp.float32
    )
    return first_position + jnp.einsum(
        "ol,wld->wod", divide_pair_table[1], input_values, preferred_element_type=jnp.float32
    )


def group_size():
    return 4


def body(signal, gate, filt, bias, doc_ids, block_perm, out_weight):
    block_len = SPAN
    frame_len = 2 * block_len
    channels = signal.shape[1]
    highest_index = lax.Precision.HIGHEST
    whole_filter = lax.all_gather(filt, "ctx", axis=0, tiled=True)
    positions = jnp.arange(frame_len, dtype=jnp.int32)
    phase_idx = positions[:, None] * positions[None, :] % frame_len
    angles = phase_idx.astype(jnp.float32) * (2.0 * math.pi / frame_len)
    cos_tab = jnp.cos(angles)
    sin_tab = jnp.sin(angles)
    cos_kernel = split_table(cos_tab[:, : frame_len - 1])
    sin_kernel = split_table(sin_tab[:, : frame_len - 1])
    cos_source = split_table(cos_tab[:, :block_len])
    sine_source_rows = split_table(sin_tab[:, :block_len])
    cycle_pos = lax.axis_index("ctx")
    own_blocks = lax.dynamic_slice_in_dim(block_perm, 2 * cycle_pos, 2)
    target_blocks = [own_blocks[0], own_blocks[1]]
    target_docs = [
        lax.dynamic_slice_in_dim(doc_ids, number * block_len, block_len) for number in target_blocks
    ]
    lead_docs = [docs[0] for docs in target_docs]
    own_rows = [signal[:block_len], signal[block_len:]]

    def block_docs(number):
        return lax.dynamic_slice_in_dim(doc_ids, number * block_len, block_len)

    def filter_window(lag_blocks):
        return lax.dynamic_slice_in_dim(
            whole_filter, lag_blocks * block_len - block_len + 1, frame_len - 1, 0
        )

    def pair_spectra(sources, source_numbers, target_numbers, leads):
        source_docs = jax.vmap(block_docs)(source_numbers)
        keep_rows = (source_docs == leads[:, None]) & (source_numbers < target_numbers)[:, None]
        masked = jnp.where(keep_rows[:, :, None], sources, jnp.zeros_like(sources))
        lag_blocks = jnp.maximum(target_numbers - source_numbers, 1)
        windows = jax.vmap(filter_window)(lag_blocks)
        kernel_re = transform_many(cos_kernel, windows)
        kernel_im = -transform_many(sin_kernel, windows)
        source_re = transform_many(cos_source, masked)
        source_im = -transform_many(sine_source_rows, masked)
        return (
            kernel_re * source_re - kernel_im * source_im,
            kernel_re * source_im + kernel_im * source_re,
        )

    def inverse(spec_re, spec_im, docs, lead_doc):
        values = jnp.dot(cos_tab[block_len - 1 : frame_len - 1], spec_re, precision=highest_index)
        values = values - jnp.dot(
            sin_tab[block_len - 1 : frame_len - 1], spec_im, precision=highest_index
        )
        return jnp.where((docs == lead_doc)[:, None], values / frame_len, 0.0)

    zero_spec = jnp.zeros((frame_len, channels), jnp.float32)
    totals = (zero_spec, zero_spec, zero_spec, zero_spec)
    arrived = lax.all_gather(signal, "ctx", axis=0, tiled=True)
    block_count = arrived.shape[0] // block_len
    group = group_size()
    steps = block_count // group
    arrived_groups = arrived.reshape(steps, group, block_len, channels)

    def absorb_group(running, item):
        group_rows, step_index = item
        numbers = lax.dynamic_slice_in_dim(block_perm, step_index * group, group)
        sources = jnp.concatenate([group_rows, group_rows], axis=0)
        source_numbers = jnp.concatenate([numbers, numbers], axis=0)
        target_numbers = jnp.concatenate(
            [
                jnp.full((group,), target_blocks[0], jnp.int32),
                jnp.full((group,), target_blocks[1], jnp.int32),
            ],
            axis=0,
        )
        leads = jnp.concatenate(
            [
                jnp.full((group,), lead_docs[0], jnp.int32),
                jnp.full((group,), lead_docs[1], jnp.int32),
            ],
            axis=0,
        )
        part_re, part_im = pair_spectra(sources, source_numbers, target_numbers, leads)
        part_re = part_re.reshape(2, group, frame_len, channels).sum(axis=1)
        part_im = part_im.reshape(2, group, frame_len, channels).sum(axis=1)
        return (
            (
                running[0] + part_re[0],
                running[1] + part_im[0],
                running[2] + part_re[1],
                running[3] + part_im[1],
            ),
            None,
        )

    totals, unused = lax.scan(
        absorb_group, totals, (arrived_groups, jnp.arange(steps, dtype=jnp.int32))
    )
    distant = [
        inverse(totals[2 * slot], totals[2 * slot + 1], target_docs[slot], lead_docs[slot])
        for slot in range(2)
    ]
    offsets = positions[:block_len][:, None] - positions[:block_len][None, :]
    near_taps = whole_filter[:block_len]
    gathered_taps = near_taps[jnp.maximum(offsets, 0)]
    gated_parts = []
    for slot in range(2):
        docs = target_docs[slot]
        allowed = (offsets >= 0) & (docs[:, None] == docs[None, :])
        toeplitz = jnp.where(allowed[:, :, None], gathered_taps, jnp.zeros_like(gathered_taps))
        local_part = jnp.einsum(
            "tsc,sc->tc", toeplitz, own_rows[slot], preferred_element_type=jnp.float32
        )
        source = own_rows[slot].astype(jnp.float32)
        gate_rows = gate[slot * block_len : (slot + 1) * block_len].astype(jnp.float32)
        gated_parts.append(
            (gate_rows * (local_part + distant[slot] + bias[None, :] * source)).astype(jnp.bfloat16)
        )
    gated = jnp.concatenate(gated_parts, axis=0)
    partial_value = jnp.dot(gated, out_weight, preferred_element_type=jnp.float32)
    return lax.psum_scatter(partial_value, "tp", scatter_dimension=1, tiled=True).astype(
        jnp.bfloat16
    )


def solution(mesh):
    return jax.shard_map(
        body,
        mesh=mesh,
        in_specs=(P("ctx", "tp"), P("ctx", "tp"), P("ctx", "tp"), P("tp"), P(), P(), P("tp", None)),
        out_specs=P("ctx", "tp"),
        check_vma=False,
    )
```

profile of v0, /device:TPU:1, one launch (start us, length us, event | category | flops | bytes accessed | tf_op | source)
XLA Modules:
  0.0 1316.1 jit_solution(3132769725770774739)
XLA Ops:
  22.6 127.1 %all-gather.3.cloned.1.call-done = bf16[4096,512]{1,0:T(8,128)(2,1)} async-done(((bf16[128,512]{1,0:T(8,128)(2,1)}), bf16[4096,512]{1,0:T(8,128)(2,1)}) %all-gather.3.cloned.1.call-update) | async-done | bytes 4194320 | tf_op jit(solution)/shard_map/all_gather | solution.py:34
  149.7 158.3 %all-gather.5.cloned.1.call-done = bf16[4096,512]{1,0:T(8,128)(2,1)} async-done(((bf16[128,512]{1,0:T(8,128)(2,1)}), bf16[4096,512]{1,0:T(8,128)(2,1)}) %all-gather.5.cloned.1.call-update) | async-done | bytes 4194320 | tf_op jit(solution)/shard_map/all_gather | solution.py:85
  308.5 916.3 %while.29 = (s32[]{:T(128)}, f32[128,512]{0,1:T(8,128)}, f32[128,512]{0,1:T(8,128)}, f32[128,512]{0,1:T(8,128)}, f32[128,512]{0,1:T(8,128)}, /*index=5*/s32[]{:T...) while((s32[]{:T(128)}, f32[128,512]{0,1:T(8,128)}, ...), condition=%wide.region_3.4_spmd.clone, body=%wide.region_0.3_spmd.clone.sunk | while | flops 810812544 | bytes 56596156 | solution.py:123
  312.6 17.9 %while.30 = (s32[]{:T(128)}, bf16[4096,512]{1,0:T(8,128)(2,1)}, s32[8,2]{0,1:T(2,128)S(1)}, bf16[8,127,512]{2,1,0:T(8,128)(2,1)S(1)}, s32[]{:T(128)}) while((s32[]{:T(128)}, bf16[4096,512]{1,0:T(8,128)(2,1)}, s32[8,2]{0,1:T(2,128)S(1)}, bf16[8,127,512]{2,1,0:T(8,128)(2,1)S(1)}, s32[]{:T(128)}) %tuple.94), condition=%wide.while_cond, body=%wide.while_body.sunk | while | flops 2 | bytes 261225 | solution.py:57
  368.8 17.9 %while.30 = (s32[]{:T(128)}, bf16[4096,512]{1,0:T(8,128)(2,1)}, s32[8,2]{0,1:T(2,128)S(1)}, bf16[8,127,512]{2,1,0:T(8,128)(2,1)S(1)}, s32[]{:T(128)}) while((s32[]{:T(128)}, bf16[4096,512]{1,0:T(8,128)(2,1)}, s32[8,2]{0,1:T(2,128)S(1)}, bf16[8,127,512]{2,1,0:T(8,128)(2,1)S(1)}, s32[]{:T(128)}) %tuple.94), condition=%wide.while_cond, body=%wide.while_body.sunk | while | flops 2 | bytes 261225 | solution.py:57
  426.2 17.9 %while.30 = (s32[]{:T(128)}, bf16[4096,512]{1,0:T(8,128)(2,1)}, s32[8,2]{0,1:T(2,128)S(1)}, bf16[8,127,512]{2,1,0:T(8,128)(2,1)S(1)}, s32[]{:T(128)}) while((s32[]{:T(128)}, bf16[4096,512]{1,0:T(8,128)(2,1)}, s32[8,2]{0,1:T(2,128)S(1)}, bf16[8,127,512]{2,1,0:T(8,128)(2,1)S(1)}, s32[]{:T(128)}) %tuple.94), condition=%wide.while_cond, body=%wide.while_body.sunk | while | flops 2 | bytes 261225 | solution.py:57
  483.5 17.9 %while.30 = (s32[]{:T(128)}, bf16[4096,512]{1,0:T(8,128)(2,1)}, s32[8,2]{0,1:T(2,128)S(1)}, bf16[8,127,512]{2,1,0:T(8,128)(2,1)S(1)}, s32[]{:T(128)}) while((s32[]{:T(128)}, bf16[4096,512]{1,0:T(8,128)(2,1)}, s32[8,2]{0,1:T(2,128)S(1)}, bf16[8,127,512]{2,1,0:T(8,128)(2,1)S(1)}, s32[]{:T(128)}) %tuple.94), condition=%wide.while_cond, body=%wide.while_body.sunk | while | flops 2 | bytes 261225 | solution.py:57
  540.8 17.9 %while.30 = (s32[]{:T(128)}, bf16[4096,512]{1,0:T(8,128)(2,1)}, s32[8,2]{0,1:T(2,128)S(1)}, bf16[8,127,512]{2,1,0:T(8,128)(2,1)S(1)}, s32[]{:T(128)}) while((s32[]{:T(128)}, bf16[4096,512]{1,0:T(8,128)(2,1)}, s32[8,2]{0,1:T(2,128)S(1)}, bf16[8,127,512]{2,1,0:T(8,128)(2,1)S(1)}, s32[]{:T(128)}) %tuple.94), condition=%wide.while_cond, body=%wide.while_body.sunk | while | flops 2 | bytes 261225 | solution.py:57
  598.2 17.9 %while.30 = (s32[]{:T(128)}, bf16[4096,512]{1,0:T(8,128)(2,1)}, s32[8,2]{0,1:T(2,128)S(1)}, bf16[8,127,512]{2,1,0:T(8,128)(2,1)S(1)}, s32[]{:T(128)}) while((s32[]{:T(128)}, bf16[4096,512]{1,0:T(8,128)(2,1)}, s32[8,2]{0,1:T(2,128)S(1)}, bf16[8,127,512]{2,1,0:T(8,128)(2,1)S(1)}, s32[]{:T(128)}) %tuple.94), condition=%wide.while_cond, body=%wide.while_body.sunk | while | flops 2 | bytes 261225 | solution.py:57
  655.5 17.9 %while.30 = (s32[]{:T(128)}, bf16[4096,512]{1,0:T(8,128)(2,1)}, s32[8,2]{0,1:T(2,128)S(1)}, bf16[8,127,512]{2,1,0:T(8,128)(2,1)S(1)}, s32[]{:T(128)}) while((s32[]{:T(128)}, bf16[4096,512]{1,0:T(8,128)(2,1)}, s32[8,2]{0,1:T(2,128)S(1)}, bf16[8,127,512]{2,1,0:T(8,128)(2,1)S(1)}, s32[]{:T(128)}) %tuple.94), condition=%wide.while_cond, body=%wide.while_body.sunk | while | flops 2 | bytes 261225 | solution.py:57
  682.2 17.1 %while.31 = (s32[]{:T(128)}, s32[4096]{0:T(1024)}, s32[8,1]{0,1:T(1,128)S(1)}, s32[8,64]{1,0:T(8,128)S(1)}, s32[]{:T(128)}, /*index=5*/s32[]{:T(128)}) while((s32[]{:T(128)}, s32[4096]{0:T(1024)}, s32[8,1]{0,1:T(1,128)S(1)}, s32[8,64]{1,0:T(8,128)S(1)}, s32[]{:T(128)}, /*index=5*/s32[]{:T(128)}) %tuple.97), condition=%wide.while_cond.1, body=%wide.while_body.1.sunk | while | flops 2 | bytes 1121 | solution.py:54
  712.9 17.9 %while.30 = (s32[]{:T(128)}, bf16[4096,512]{1,0:T(8,128)(2,1)}, s32[8,2]{0,1:T(2,128)S(1)}, bf16[8,127,512]{2,1,0:T(8,128)(2,1)S(1)}, s32[]{:T(128)}) while((s32[]{:T(128)}, bf16[4096,512]{1,0:T(8,128)(2,1)}, s32[8,2]{0,1:T(2,128)S(1)}, bf16[8,127,512]{2,1,0:T(8,128)(2,1)S(1)}, s32[]{:T(128)}) %tuple.94), condition=%wide.while_cond, body=%wide.while_body.sunk | while | flops 2 | bytes 261225 | solution.py:57
  739.6 17.1 %while.31 = (s32[]{:T(128)}, s32[4096]{0:T(1024)}, s32[8,1]{0,1:T(1,128)S(1)}, s32[8,64]{1,0:T(8,128)S(1)}, s32[]{:T(128)}, /*index=5*/s32[]{:T(128)}) while((s32[]{:T(128)}, s32[4096]{0:T(1024)}, s32[8,1]{0,1:T(1,128)S(1)}, s32[8,64]{1,0:T(8,128)S(1)}, s32[]{:T(128)}, /*index=5*/s32[]{:T(128)}) %tuple.97), condition=%wide.while_cond.1, body=%wide.while_body.1.sunk | while | flops 2 | bytes 1121 | solution.py:54
  770.3 17.9 %while.30 = (s32[]{:T(128)}, bf16[4096,512]{1,0:T(8,128)(2,1)}, s32[8,2]{0,1:T(2,128)S(1)}, bf16[8,127,512]{2,1,0:T(8,128)(2,1)S(1)}, s32[]{:T(128)}) while((s32[]{:T(128)}, bf16[4096,512]{1,0:T(8,128)(2,1)}, s32[8,2]{0,1:T(2,128)S(1)}, bf16[8,127,512]{2,1,0:T(8,128)(2,1)S(1)}, s32[]{:T(128)}) %tuple.94), condition=%wide.while_cond, body=%wide.while_body.sunk | while | flops 2 | bytes 261225 | solution.py:57
  827.6 17.9 %while.30 = (s32[]{:T(128)}, bf16[4096,512]{1,0:T(8,128)(2,1)}, s32[8,2]{0,1:T(2,128)S(1)}, bf16[8,127,512]{2,1,0:T(8,128)(2,1)S(1)}, s32[]{:T(128)}) while((s32[]{:T(128)}, bf16[4096,512]{1,0:T(8,128)(2,1)}, s32[8,2]{0,1:T(2,128)S(1)}, bf16[8,127,512]{2,1,0:T(8,128)(2,1)S(1)}, s32[]{:T(128)}) %tuple.94), condition=%wide.while_cond, body=%wide.while_body.sunk | while | flops 2 | bytes 261225 | solution.py:57
  854.3 17.1 %while.31 = (s32[]{:T(128)}, s32[4096]{0:T(1024)}, s32[8,1]{0,1:T(1,128)S(1)}, s32[8,64]{1,0:T(8,128)S(1)}, s32[]{:T(128)}, /*index=5*/s32[]{:T(128)}) while((s32[]{:T(128)}, s32[4096]{0:T(1024)}, s32[8,1]{0,1:T(1,128)S(1)}, s32[8,64]{1,0:T(8,128)S(1)}, s32[]{:T(128)}, /*index=5*/s32[]{:T(128)}) %tuple.97), condition=%wide.while_cond.1, body=%wide.while_body.1.sunk | while | flops 2 | bytes 1121 | solution.py:54
  885.0 17.9 %while.30 = (s32[]{:T(128)}, bf16[4096,512]{1,0:T(8,128)(2,1)}, s32[8,2]{0,1:T(2,128)S(1)}, bf16[8,127,512]{2,1,0:T(8,128)(2,1)S(1)}, s32[]{:T(128)}) while((s32[]{:T(128)}, bf16[4096,512]{1,0:T(8,128)(2,1)}, s32[8,2]{0,1:T(2,128)S(1)}, bf16[8,127,512]{2,1,0:T(8,128)(2,1)S(1)}, s32[]{:T(128)}) %tuple.94), condition=%wide.while_cond, body=%wide.while_body.sunk | while | flops 2 | bytes 261225 | solution.py:57
  942.3 17.9 %while.30 = (s32[]{:T(128)}, bf16[4096,512]{1,0:T(8,128)(2,1)}, s32[8,2]{0,1:T(2,128)S(1)}, bf16[8,127,512]{2,1,0:T(8,128)(2,1)S(1)}, s32[]{:T(128)}) while((s32[]{:T(128)}, bf16[4096,512]{1,0:T(8,128)(2,1)}, s32[8,2]{0,1:T(2,128)S(1)}, bf16[8,127,512]{2,1,0:T(8,128)(2,1)S(1)}, s32[]{:T(128)}) %tuple.94), condition=%wide.while_cond, body=%wide.while_body.sunk | while | flops 2 | bytes 261225 | solution.py:57
  999.6 17.9 %while.30 = (s32[]{:T(128)}, bf16[4096,512]{1,0:T(8,128)(2,1)}, s32[8,2]{0,1:T(2,128)S(1)}, bf16[8,127,512]{2,1,0:T(8,128)(2,1)S(1)}, s32[]{:T(128)}) while((s32[]{:T(128)}, bf16[4096,512]{1,0:T(8,128)(2,1)}, s32[8,2]{0,1:T(2,128)S(1)}, bf16[8,127,512]{2,1,0:T(8,128)(2,1)S(1)}, s32[]{:T(128)}) %tuple.94), condition=%wide.while_cond, body=%wide.while_body.sunk | while | flops 2 | bytes 261225 | solution.py:57
  1057.0 17.9 %while.30 = (s32[]{:T(128)}, bf16[4096,512]{1,0:T(8,128)(2,1)}, s32[8,2]{0,1:T(2,128)S(1)}, bf16[8,127,512]{2,1,0:T(8,128)(2,1)S(1)}, s32[]{:T(128)}) while((s32[]{:T(128)}, bf16[4096,512]{1,0:T(8,128)(2,1)}, s32[8,2]{0,1:T(2,128)S(1)}, bf16[8,127,512]{2,1,0:T(8,128)(2,1)S(1)}, s32[]{:T(128)}) %tuple.94), condition=%wide.while_cond, body=%wide.while_body.sunk | while | flops 2 | bytes 261225 | solution.py:57
  1114.3 17.9 %while.30 = (s32[]{:T(128)}, bf16[4096,512]{1,0:T(8,128)(2,1)}, s32[8,2]{0,1:T(2,128)S(1)}, bf16[8,127,512]{2,1,0:T(8,128)(2,1)S(1)}, s32[]{:T(128)}) while((s32[]{:T(128)}, bf16[4096,512]{1,0:T(8,128)(2,1)}, s32[8,2]{0,1:T(2,128)S(1)}, bf16[8,127,512]{2,1,0:T(8,128)(2,1)S(1)}, s32[]{:T(128)}) %tuple.94), condition=%wide.while_cond, body=%wide.while_body.sunk | while | flops 2 | bytes 261225 | solution.py:57
  1171.7 17.9 %while.30 = (s32[]{:T(128)}, bf16[4096,512]{1,0:T(8,128)(2,1)}, s32[8,2]{0,1:T(2,128)S(1)}, bf16[8,127,512]{2,1,0:T(8,128)(2,1)S(1)}, s32[]{:T(128)}) while((s32[]{:T(128)}, bf16[4096,512]{1,0:T(8,128)(2,1)}, s32[8,2]{0,1:T(2,128)S(1)}, bf16[8,127,512]{2,1,0:T(8,128)(2,1)S(1)}, s32[]{:T(128)}) %tuple.94), condition=%wide.while_cond, body=%wide.while_body.sunk | while | flops 2 | bytes 261225 | solution.py:57
  1228.7 18.7 %gather_fusion = bf16[4096,512]{1,0:T(8,128)(2,1)} fusion(bf16[64,512]{1,0:T(8,128)(2,1)S(1)} %slice.146, s32[4096]{0:T(1024)} %broadcast_clamp_fusion), kind=kCustom, calls=%fused_computation | custom fusion | bytes 8404992 | tf_op jit(solution)/shard_map/gather | solution.py:132
  1256.1 51.8 %reduce-scatter.2.cloned.1.call-done = f32[128,512]{1,0:T(8,128)} async-done(((f32[128,2048]{1,0:T(8,128)}), f32[128,512]{1,0:T(8,128)}) %reduce-scatter.2.cloned.1.call-update) | async-done | bytes 262160 | tf_op jit(solution)/shard_map/reduce_scatter | solution.py:148
  (1339 shorter events, 1152.1 us)
Async XLA Ops:
  6.5 1248.1 %copy-start = (bf16[512,2048]{1,0:T(8,128)(2,1)S(1)}, bf16[512,2048]{1,0:T(8,128)(2,1)}, u32[]{:S(2)}) copy-start(bf16[512,2048]{1,0:T(8,128)(2,1)} %param.15) | copy-start | bytes 6291460
  6.5 143.2 %all-gather.3.cloned.1.call-start = ((), (), s32[]{:S(2)}) async-start(), calls=%async_computation.1 | async-start | bytes 4325376 | tf_op jit(solution)/shard_map/all_gather | solution.py:34
  7.3 300.7 %all-gather.5.cloned.1.call-start = ((), (), s32[]{:S(2)}) async-start(), calls=%async_computation.2 | async-start | bytes 4325376 | tf_op jit(solution)/shard_map/all_gather | solution.py:85
  8.0 1299.9 %reduce-scatter.2.cloned.1.call-start = ((), (), s32[]{:S(2)}) async-start(), calls=%async_computation.3 | async-start | bytes 1310720 | tf_op jit(solution)/shard_map/reduce_scatter | solution.py:148
  335.6 3.6 copy-start.15
  391.8 3.6 copy-start.15
  449.1 3.6 copy-start.15
  735.9 3.6 copy-start.15
  965.3 3.6 copy-start.15
  1022.6 3.6 copy-start.15
  1079.9 3.6 copy-start.15
  1137.3 3.6 copy-start.15
  1194.6 3.6 copy-start.15
  1228.6 18.8 %copy-start.7 = (f32[512,64]{0,1:T(8,128)S(1)}, f32[512,64]{0,1:T(8,128)}, u32[]{:S(2)}) copy-start(f32[512,64]{0,1:T(8,128)} %get-tuple-element.671) | copy-start | bytes 393220
  1228.6 18.8 %copy-start.8 = (f32[512,64]{0,1:T(8,128)S(1)}, f32[512,64]{0,1:T(8,128)}, u32[]{:S(2)}) copy-start(f32[512,64]{0,1:T(8,128)} %get-tuple-element.672) | copy-start | bytes 393220
  1228.6 18.8 %copy-start.10 = (pred[64,64]{1,0:T(8,128)(4,1)S(1)}, pred[64,64]{1,0:T(8,128)(4,1)}, u32[]{:S(2)}) copy-start(pred[64,64]{1,0:T(8,128)(4,1)} %get-tuple-element.675) | copy-start | bytes 12292
  1228.6 18.7 %copy-start.11 = (pred[64,64]{1,0:T(8,128)(4,1)S(1)}, pred[64,64]{1,0:T(8,128)(4,1)}, u32[]{:S(2)}) copy-start(pred[64,64]{1,0:T(8,128)(4,1)} %get-tuple-element.676) | copy-start | bytes 12292
  1247.4 6.1 copy-start.4
  1247.4 6.1 copy-start.5
  1247.4 6.1 copy-start.9
  1247.4 6.1 copy-start.12
  1247.4 6.1 copy-start.14
  1247.5 6.6 copy-start.3
  1247.5 6.6 copy-start.13
  (55 other events, 116.5 us)
Sparse Core Ops, SparseCore 0:
  9.0 140.6 all-gather.2
  151.3 156.5 all-gather.4
  1256.2 51.6 reduce-scatter.1
where the time goes:
time: 1330 us; the launch traced here: 1320 us
  local copies, waits for them, and re-layouts  666 us (50%)
  waiting for transfers between devices  339 us (25%)
  matrix products  204 us (15%)
  other arithmetic  77.2 us (6%)
  loops' own time  15.1 us (1%)
  between operations  14.7 us (1%)
    gather x768, local copies, waits for them, and re-layouts  556 us
    all_gather x1, waiting for transfers between devices, body(): arrived = lax.all_gather(signal, 'ctx', axis=0, tiled=True)  158 us
    all_gather x1, waiting for transfers between devices, body(): whole_filter = lax.all_gather(filt, 'ctx', axis=0, tiled=True)  127 us
    dot_general x64, matrix products, transform_many(): jnp.einsum('ol,wld->wod', divide_pair_table[1], input_values, preferred_e...  114 us
    dot_general x64, matrix products, transform_many(): jnp.einsum('ol,wld->wod', divide_pair_table[0], input_values, preferred_e...  84.9 us
    reduce_scatter x1, waiting for transfers between devices, body(): lax.psum_scatter(partial_value, 'tp', scatter_dimension=1, tiled=True)  51.8 us
    add x16, other arithmetic, absorb_group(): running[3] + part_im[1]  35.1 us
  transfers between devices with their start and end apart: 3, of which 3 were waited for; matrix products, arithmetic and copies ran while one was open for 1% of the time, Pallas kernels for 0%

commit v1 on v0

--- a/solution.py
+++ b/solution.py
@@ -5,6 +5,9 @@
 from jax.sharding import PartitionSpec as P
 
 SPAN = 64
+wait_lane = lambda local_values: jnp.concatenate(
+    lax.all_to_all(jnp.stack([local_values] * lax.axis_size("ctx"), axis=0), "ctx", 0, 0), 0
+)
 
 
 def split_table(table):
@@ -82,7 +85,7 @@
 
     zero_spec = jnp.zeros((frame_len, channels), jnp.float32)
     totals = (zero_spec, zero_spec, zero_spec, zero_spec)
-    arrived = lax.all_gather(signal, "ctx", axis=0, tiled=True)
+    arrived = wait_lane(signal)
     block_count = arrived.shape[0] // block_len
     group = group_size()
     steps = block_count // group

time: 1330 us -> 1110 us (0.83)
  waiting for transfers between devices: 339 us -> 212 us
  matrix products: 204 us -> 143 us
  local copies, waits for them, and re-layouts: 666 us -> 627 us
    all_gather x1 -> x0, waiting for transfers between devices: 158 us -> none  [body(): arrived = lax.all_gather(signal, 'ctx', axis=0, tiled=True)]
    all_to_all x0 -> x1, waiting for transfers between devices: none -> 59 us  [lax.all_to_all(jnp.stack([local_values] * lax.axis_size('ctx'), axis=0),...]
    dot_general x64, matrix products: 114 us -> 79 us  [transform_many(): jnp.einsum('ol,wld->wod', divide_pair_table[1], input_values, preferred_e...]
    dot_general x64, matrix products: 84.9 us -> 59.1 us  [transform_many(): jnp.einsum('ol,wld->wod', divide_pair_table[0], input_values, preferred_e...]
    all_gather x1, waiting for transfers between devices: 127 us -> 104 us  [body(): whole_filter = lax.all_gather(filt, 'ctx', axis=0, tiled=True)]
    while x128 -> x416, local copies, waits for them, and re-layouts: 3.9 us -> 20.1 us
    gather x768, local copies, waits for them, and re-layouts: 556 us -> 541 us
where the time goes in v1:
time: 1110 us; the launch traced here: 1090 us
  local copies, waits for them, and re-layouts  627 us (56%)
  waiting for transfers between devices  212 us (19%)
  matrix products  143 us (13%)
  other arithmetic  70.3 us (6%)
  loops' own time  16.8 us (2%)
  between operations  14.9 us (1%)
    gather x768, local copies, waits for them, and re-layouts  541 us
    all_gather x1, waiting for transfers between devices, body(): whole_filter = lax.all_gather(filt, 'ctx', axis=0, tiled=True)  104 us
    dot_general x64, matrix products, transform_many(): jnp.einsum('ol,wld->wod', divide_pair_table[1], input_values, preferred_e...  79 us
    dot_general x64, matrix products, transform_many(): jnp.einsum('ol,wld->wod', divide_pair_table[0], input_values, preferred_e...  59.1 us
    all_to_all x1, waiting for transfers between devices, lax.all_to_all(jnp.stack([local_values] * lax.axis_size('ctx'), axis=0),...  59 us
    reduce_scatter x1, waiting for transfers between devices, body(): lax.psum_scatter(partial_value, 'tp', scatter_dimension=1, tiled=True)  48.4 us
    add x16, other arithmetic, absorb_group(): running[3] + part_im[1]  34.4 us
  transfers between devices with their start and end apart: 3, of which 3 were waited for; matrix products, arithmetic and copies ran while one was open for 1% of the time, Pallas kernels for 0%

profile of v1, /device:TPU:1, one launch (start us, length us, event | category | flops | bytes accessed | tf_op | source)
XLA Modules:
  0.0 1094.8 jit_solution(9339278396753289499)
XLA Ops:
  30.3 59.0 %all-to-all-done = bf16[32,128,512]{2,1,0:T(8,128)(2,1)} async-done(((bf16[32,128,512]{2,1,0:T(8,128)(2,1)}), bf16[32,128,512]{2,1,0:T(8,128)(2,1)}, u32[]{:S(2)}, u32[]{:S(2)}) %all-to-all-start) | async-done | bytes 4194336 | tf_op jit(solution)/shard_map/all_to_all | solution.py:9
  89.3 104.0 %all-gather.2.cloned.1.call-done = bf16[4096,512]{1,0:T(8,128)(2,1)} async-done(((bf16[128,512]{1,0:T(8,128)(2,1)}), bf16[4096,512]{1,0:T(8,128)(2,1)}) %all-gather.2.cloned.1.call-update) | async-done | bytes 4194320 | tf_op jit(solution)/shard_map/all_gather | solution.py:37
  193.3 813.5 %while.29 = (s32[]{:T(128)}, f32[128,512]{0,1:T(8,128)}, f32[128,512]{0,1:T(8,128)}, f32[128,512]{0,1:T(8,128)}, f32[128,512]{0,1:T(8,128)}, /*index=5*/s32[]{:T...) while((s32[]{:T(128)}, f32[128,512]{0,1:T(8,128)}, ...), condition=%wide.region_3.4_spmd.clone, body=%wide.region_0.3_spmd.clone.sunk | while | flops 810812544 | bytes 48664040 | solution.py:126
  218.4 17.7 %while.30 = (s32[]{:T(128)}, bf16[4096,512]{1,0:T(8,128)(2,1)}, s32[8,2]{0,1:T(2,128)S(1)}, bf16[8,127,512]{2,1,0:T(8,128)(2,1)S(1)}, s32[]{:T(128)}) while((s32[]{:T(128)}, bf16[4096,512]{1,0:T(8,128)(2,1)}, s32[8,2]{0,1:T(2,128)S(1)}, bf16[8,127,512]{2,1,0:T(8,128)(2,1)S(1)}, s32[]{:T(128)}) %tuple.94), condition=%wide.while_cond, body=%wide.while_body.sunk | while | flops 2 | bytes 261217 | solution.py:60
  268.1 17.7 %while.30 = (s32[]{:T(128)}, bf16[4096,512]{1,0:T(8,128)(2,1)}, s32[8,2]{0,1:T(2,128)S(1)}, bf16[8,127,512]{2,1,0:T(8,128)(2,1)S(1)}, s32[]{:T(128)}) while((s32[]{:T(128)}, bf16[4096,512]{1,0:T(8,128)(2,1)}, s32[8,2]{0,1:T(2,128)S(1)}, bf16[8,127,512]{2,1,0:T(8,128)(2,1)S(1)}, s32[]{:T(128)}) %tuple.94), condition=%wide.while_cond, body=%wide.while_body.sunk | while | flops 2 | bytes 261217 | solution.py:60
  319.0 17.7 %while.30 = (s32[]{:T(128)}, bf16[4096,512]{1,0:T(8,128)(2,1)}, s32[8,2]{0,1:T(2,128)S(1)}, bf16[8,127,512]{2,1,0:T(8,128)(2,1)S(1)}, s32[]{:T(128)}) while((s32[]{:T(128)}, bf16[4096,512]{1,0:T(8,128)(2,1)}, s32[8,2]{0,1:T(2,128)S(1)}, bf16[8,127,512]{2,1,0:T(8,128)(2,1)S(1)}, s32[]{:T(128)}) %tuple.94), condition=%wide.while_cond, body=%wide.while_body.sunk | while | flops 2 | bytes 261217 | solution.py:60
  369.9 17.7 %while.30 = (s32[]{:T(128)}, bf16[4096,512]{1,0:T(8,128)(2,1)}, s32[8,2]{0,1:T(2,128)S(1)}, bf16[8,127,512]{2,1,0:T(8,128)(2,1)S(1)}, s32[]{:T(128)}) while((s32[]{:T(128)}, bf16[4096,512]{1,0:T(8,128)(2,1)}, s32[8,2]{0,1:T(2,128)S(1)}, bf16[8,127,512]{2,1,0:T(8,128)(2,1)S(1)}, s32[]{:T(128)}) %tuple.94), condition=%wide.while_cond, body=%wide.while_body.sunk | while | flops 2 | bytes 261217 | solution.py:60
  420.9 17.7 %while.30 = (s32[]{:T(128)}, bf16[4096,512]{1,0:T(8,128)(2,1)}, s32[8,2]{0,1:T(2,128)S(1)}, bf16[8,127,512]{2,1,0:T(8,128)(2,1)S(1)}, s32[]{:T(128)}) while((s32[]{:T(128)}, bf16[4096,512]{1,0:T(8,128)(2,1)}, s32[8,2]{0,1:T(2,128)S(1)}, bf16[8,127,512]{2,1,0:T(8,128)(2,1)S(1)}, s32[]{:T(128)}) %tuple.94), condition=%wide.while_cond, body=%wide.while_body.sunk | while | flops 2 | bytes 261217 | solution.py:60
  449.5 16.3 %while.31 = (s32[]{:T(128)}, s32[4096]{0:T(1024)}, s32[8,1]{0,1:T(1,128)S(1)}, s32[8,64]{1,0:T(8,128)S(1)}, s32[]{:T(128)}, /*index=5*/s32[]{:T(128)}) while((s32[]{:T(128)}, s32[4096]{0:T(1024)}, s32[8,1]{0,1:T(1,128)S(1)}, s32[8,64]{1,0:T(8,128)S(1)}, s32[]{:T(128)}, /*index=5*/s32[]{:T(128)}) %tuple.97), condition=%wide.while_cond.1, body=%wide.while_body.1.sunk | while | flops 2 | bytes 1113 | solution.py:57
  471.8 17.7 %while.30 = (s32[]{:T(128)}, bf16[4096,512]{1,0:T(8,128)(2,1)}, s32[8,2]{0,1:T(2,128)S(1)}, bf16[8,127,512]{2,1,0:T(8,128)(2,1)S(1)}, s32[]{:T(128)}) while((s32[]{:T(128)}, bf16[4096,512]{1,0:T(8,128)(2,1)}, s32[8,2]{0,1:T(2,128)S(1)}, bf16[8,127,512]{2,1,0:T(8,128)(2,1)S(1)}, s32[]{:T(128)}) %tuple.94), condition=%wide.while_cond, body=%wide.while_body.sunk | while | flops 2 | bytes 261217 | solution.py:60
  500.5 16.3 %while.31 = (s32[]{:T(128)}, s32[4096]{0:T(1024)}, s32[8,1]{0,1:T(1,128)S(1)}, s32[8,64]{1,0:T(8,128)S(1)}, s32[]{:T(128)}, /*index=5*/s32[]{:T(128)}) while((s32[]{:T(128)}, s32[4096]{0:T(1024)}, s32[8,1]{0,1:T(1,128)S(1)}, s32[8,64]{1,0:T(8,128)S(1)}, s32[]{:T(128)}, /*index=5*/s32[]{:T(128)}) %tuple.97), condition=%wide.while_cond.1, body=%wide.while_body.1.sunk | while | flops 2 | bytes 1113 | solution.py:57
  522.7 17.7 %while.30 = (s32[]{:T(128)}, bf16[4096,512]{1,0:T(8,128)(2,1)}, s32[8,2]{0,1:T(2,128)S(1)}, bf16[8,127,512]{2,1,0:T(8,128)(2,1)S(1)}, s32[]{:T(128)}) while((s32[]{:T(128)}, bf16[4096,512]{1,0:T(8,128)(2,1)}, s32[8,2]{0,1:T(2,128)S(1)}, bf16[8,127,512]{2,1,0:T(8,128)(2,1)S(1)}, s32[]{:T(128)}) %tuple.94), condition=%wide.while_cond, body=%wide.while_body.sunk | while | flops 2 | bytes 261217 | solution.py:60
  573.7 17.7 %while.30 = (s32[]{:T(128)}, bf16[4096,512]{1,0:T(8,128)(2,1)}, s32[8,2]{0,1:T(2,128)S(1)}, bf16[8,127,512]{2,1,0:T(8,128)(2,1)S(1)}, s32[]{:T(128)}) while((s32[]{:T(128)}, bf16[4096,512]{1,0:T(8,128)(2,1)}, s32[8,2]{0,1:T(2,128)S(1)}, bf16[8,127,512]{2,1,0:T(8,128)(2,1)S(1)}, s32[]{:T(128)}) %tuple.94), condition=%wide.while_cond, body=%wide.while_body.sunk | while | flops 2 | bytes 261217 | solution.py:60
  624.6 17.7 %while.30 = (s32[]{:T(128)}, bf16[4096,512]{1,0:T(8,128)(2,1)}, s32[8,2]{0,1:T(2,128)S(1)}, bf16[8,127,512]{2,1,0:T(8,128)(2,1)S(1)}, s32[]{:T(128)}) while((s32[]{:T(128)}, bf16[4096,512]{1,0:T(8,128)(2,1)}, s32[8,2]{0,1:T(2,128)S(1)}, bf16[8,127,512]{2,1,0:T(8,128)(2,1)S(1)}, s32[]{:T(128)}) %tuple.94), condition=%wide.while_cond, body=%wide.while_body.sunk | while | flops 2 | bytes 261217 | solution.py:60
  653.2 16.3 %while.31 = (s32[]{:T(128)}, s32[4096]{0:T(1024)}, s32[8,1]{0,1:T(1,128)S(1)}, s32[8,64]{1,0:T(8,128)S(1)}, s32[]{:T(128)}, /*index=5*/s32[]{:T(128)}) while((s32[]{:T(128)}, s32[4096]{0:T(1024)}, s32[8,1]{0,1:T(1,128)S(1)}, s32[8,64]{1,0:T(8,128)S(1)}, s32[]{:T(128)}, /*index=5*/s32[]{:T(128)}) %tuple.97), condition=%wide.while_cond.1, body=%wide.while_body.1.sunk | while | flops 2 | bytes 1113 | solution.py:57
  675.5 17.7 %while.30 = (s32[]{:T(128)}, bf16[4096,512]{1,0:T(8,128)(2,1)}, s32[8,2]{0,1:T(2,128)S(1)}, bf16[8,127,512]{2,1,0:T(8,128)(2,1)S(1)}, s32[]{:T(128)}) while((s32[]{:T(128)}, bf16[4096,512]{1,0:T(8,128)(2,1)}, s32[8,2]{0,1:T(2,128)S(1)}, bf16[8,127,512]{2,1,0:T(8,128)(2,1)S(1)}, s32[]{:T(128)}) %tuple.94), condition=%wide.while_cond, body=%wide.while_body.sunk | while | flops 2 | bytes 261217 | solution.py:60
  726.4 17.7 %while.30 = (s32[]{:T(128)}, bf16[4096,512]{1,0:T(8,128)(2,1)}, s32[8,2]{0,1:T(2,128)S(1)}, bf16[8,127,512]{2,1,0:T(8,128)(2,1)S(1)}, s32[]{:T(128)}) while((s32[]{:T(128)}, bf16[4096,512]{1,0:T(8,128)(2,1)}, s32[8,2]{0,1:T(2,128)S(1)}, bf16[8,127,512]{2,1,0:T(8,128)(2,1)S(1)}, s32[]{:T(128)}) %tuple.94), condition=%wide.while_cond, body=%wide.while_body.sunk | while | flops 2 | bytes 261217 | solution.py:60
  777.3 17.7 %while.30 = (s32[]{:T(128)}, bf16[4096,512]{1,0:T(8,128)(2,1)}, s32[8,2]{0,1:T(2,128)S(1)}, bf16[8,127,512]{2,1,0:T(8,128)(2,1)S(1)}, s32[]{:T(128)}) while((s32[]{:T(128)}, bf16[4096,512]{1,0:T(8,128)(2,1)}, s32[8,2]{0,1:T(2,128)S(1)}, bf16[8,127,512]{2,1,0:T(8,128)(2,1)S(1)}, s32[]{:T(128)}) %tuple.94), condition=%wide.while_cond, body=%wide.while_body.sunk | while | flops 2 | bytes 261217 | solution.py:60
  828.2 17.7 %while.30 = (s32[]{:T(128)}, bf16[4096,512]{1,0:T(8,128)(2,1)}, s32[8,2]{0,1:T(2,128)S(1)}, bf16[8,127,512]{2,1,0:T(8,128)(2,1)S(1)}, s32[]{:T(128)}) while((s32[]{:T(128)}, bf16[4096,512]{1,0:T(8,128)(2,1)}, s32[8,2]{0,1:T(2,128)S(1)}, bf16[8,127,512]{2,1,0:T(8,128)(2,1)S(1)}, s32[]{:T(128)}) %tuple.94), condition=%wide.while_cond, body=%wide.while_body.sunk | while | flops 2 | bytes 261217 | solution.py:60
  879.2 17.7 %while.30 = (s32[]{:T(128)}, bf16[4096,512]{1,0:T(8,128)(2,1)}, s32[8,2]{0,1:T(2,128)S(1)}, bf16[8,127,512]{2,1,0:T(8,128)(2,1)S(1)}, s32[]{:T(128)}) while((s32[]{:T(128)}, bf16[4096,512]{1,0:T(8,128)(2,1)}, s32[8,2]{0,1:T(2,128)S(1)}, bf16[8,127,512]{2,1,0:T(8,128)(2,1)S(1)}, s32[]{:T(128)}) %tuple.94), condition=%wide.while_cond, body=%wide.while_body.sunk | while | flops 2 | bytes 261217 | solution.py:60
  930.1 17.7 %while.30 = (s32[]{:T(128)}, bf16[4096,512]{1,0:T(8,128)(2,1)}, s32[8,2]{0,1:T(2,128)S(1)}, bf16[8,127,512]{2,1,0:T(8,128)(2,1)S(1)}, s32[]{:T(128)}) while((s32[]{:T(128)}, bf16[4096,512]{1,0:T(8,128)(2,1)}, s32[8,2]{0,1:T(2,128)S(1)}, bf16[8,127,512]{2,1,0:T(8,128)(2,1)S(1)}, s32[]{:T(128)}) %tuple.94), condition=%wide.while_cond, body=%wide.while_body.sunk | while | flops 2 | bytes 261217 | solution.py:60
  981.0 17.7 %while.30 = (s32[]{:T(128)}, bf16[4096,512]{1,0:T(8,128)(2,1)}, s32[8,2]{0,1:T(2,128)S(1)}, bf16[8,127,512]{2,1,0:T(8,128)(2,1)S(1)}, s32[]{:T(128)}) while((s32[]{:T(128)}, bf16[4096,512]{1,0:T(8,128)(2,1)}, s32[8,2]{0,1:T(2,128)S(1)}, bf16[8,127,512]{2,1,0:T(8,128)(2,1)S(1)}, s32[]{:T(128)}) %tuple.94), condition=%wide.while_cond, body=%wide.while_body.sunk | while | flops 2 | bytes 261217 | solution.py:60
  1010.6 18.7 %gather_fusion = bf16[4096,512]{1,0:T(8,128)(2,1)} fusion(bf16[64,512]{1,0:T(8,128)(2,1)S(1)} %slice.146, s32[4096]{0:T(1024)} %broadcast_clamp_fusion), kind=kCustom, calls=%fused_computation | custom fusion | bytes 8404992 | tf_op jit(solution)/shard_map/gather | solution.py:135
  1037.9 48.4 %reduce-scatter.2.cloned.1.call-done = f32[128,512]{1,0:T(8,128)} async-done(((f32[128,2048]{1,0:T(8,128)}), f32[128,512]{1,0:T(8,128)}) %reduce-scatter.2.cloned.1.call-update) | async-done | bytes 262160 | tf_op jit(solution)/shard_map/reduce_scatter | solution.py:151
  (1629 shorter events, 1045.1 us)
Async XLA Ops:
  6.5 1030.0 %copy-start = (bf16[512,2048]{1,0:T(8,128)(2,1)S(1)}, bf16[512,2048]{1,0:T(8,128)(2,1)}, u32[]{:S(2)}) copy-start(bf16[512,2048]{1,0:T(8,128)(2,1)} %param.15) | copy-start | bytes 6291460
  6.5 186.8 %all-gather.2.cloned.1.call-start = ((), (), s32[]{:S(2)}) async-start(), calls=%async_computation.2 | async-start | bytes 4325376 | tf_op jit(solution)/shard_map/all_gather | solution.py:37
  10.6 78.7 %all-to-all-start = ((bf16[32,128,512]{2,1,0:T(8,128)(2,1)}), bf16[32,128,512]{2,1,0:T(8,128)(2,1)}, u32[]{:S(2)}, u32[]{:S(2)}) async-start(bf16[32,128,512]{2,1,0:T(8,128)(2,1)} %stack.2), calls=%async_computation | async-start | bytes 8388608 | tf_op jit(solution)/shard_map/all_to_all | solution.py:9
  20.6 1065.8 %reduce-scatter.2.cloned.1.call-start = ((), (), s32[]{:S(2)}) async-start(), calls=%async_computation.3 | async-start | bytes 1310720 | tf_op jit(solution)/shard_map/reduce_scatter | solution.py:151
  193.3 19.3 %copy-start.17 = (s32[]{:T(128)}, s32[]{:T(128)S(1)}, u32[]{:S(2)}) copy-start(s32[]{:T(128)S(1)} %get-tuple-element.1003) | copy-start | bytes 16 | tf_op jit(solution)/shard_map/while
  243.1 19.3 %copy-start.17 = (s32[]{:T(128)}, s32[]{:T(128)S(1)}, u32[]{:S(2)}) copy-start(s32[]{:T(128)S(1)} %get-tuple-element.1003) | copy-start | bytes 16 | tf_op jit(solution)/shard_map/while
  294.0 19.3 %copy-start.17 = (s32[]{:T(128)}, s32[]{:T(128)S(1)}, u32[]{:S(2)}) copy-start(s32[]{:T(128)S(1)} %get-tuple-element.1003) | copy-start | bytes 16 | tf_op jit(solution)/shard_map/while
  344.9 19.3 %copy-start.17 = (s32[]{:T(128)}, s32[]{:T(128)S(1)}, u32[]{:S(2)}) copy-start(s32[]{:T(128)S(1)} %get-tuple-element.1003) | copy-start | bytes 16 | tf_op jit(solution)/shard_map/while
  395.8 19.3 %copy-start.17 = (s32[]{:T(128)}, s32[]{:T(128)S(1)}, u32[]{:S(2)}) copy-start(s32[]{:T(128)S(1)} %get-tuple-element.1003) | copy-start | bytes 16 | tf_op jit(solution)/shard_map/while
  446.7 19.2 %copy-start.15 = (s32[]{:T(128)}, s32[]{:T(128)S(1)}, u32[]{:S(2)}) copy-start(s32[]{:T(128)S(1)} %get-tuple-element.1004) | copy-start | bytes 16 | tf_op jit(solution)/shard_map/while
  446.7 19.3 %copy-start.17 = (s32[]{:T(128)}, s32[]{:T(128)S(1)}, u32[]{:S(2)}) copy-start(s32[]{:T(128)S(1)} %get-tuple-element.1003) | copy-start | bytes 16 | tf_op jit(solution)/shard_map/while
  497.6 19.2 %copy-start.15 = (s32[]{:T(128)}, s32[]{:T(128)S(1)}, u32[]{:S(2)}) copy-start(s32[]{:T(128)S(1)} %get-tuple-element.1004) | copy-start | bytes 16 | tf_op jit(solution)/shard_map/while
  497.6 19.3 %copy-start.17 = (s32[]{:T(128)}, s32[]{:T(128)S(1)}, u32[]{:S(2)}) copy-start(s32[]{:T(128)S(1)} %get-tuple-element.1003) | copy-start | bytes 16 | tf_op jit(solution)/shard_map/while
  548.6 19.2 %copy-start.15 = (s32[]{:T(128)}, s32[]{:T(128)S(1)}, u32[]{:S(2)}) copy-start(s32[]{:T(128)S(1)} %get-tuple-element.1004) | copy-start | bytes 16 | tf_op jit(solution)/shard_map/while
  548.6 19.3 %copy-start.17 = (s32[]{:T(128)}, s32[]{:T(128)S(1)}, u32[]{:S(2)}) copy-start(s32[]{:T(128)S(1)} %get-tuple-element.1003) | copy-start | bytes 16 | tf_op jit(solution)/shard_map/while
  599.5 19.3 %copy-start.17 = (s32[]{:T(128)}, s32[]{:T(128)S(1)}, u32[]{:S(2)}) copy-start(s32[]{:T(128)S(1)} %get-tuple-element.1003) | copy-start | bytes 16 | tf_op jit(solution)/shard_map/while
  650.4 19.3 %copy-start.17 = (s32[]{:T(128)}, s32[]{:T(128)S(1)}, u32[]{:S(2)}) copy-start(s32[]{:T(128)S(1)} %get-tuple-element.1003) | copy-start | bytes 16 | tf_op jit(solution)/shard_map/while
  701.4 19.2 %copy-start.15 = (s32[]{:T(128)}, s32[]{:T(128)S(1)}, u32[]{:S(2)}) copy-start(s32[]{:T(128)S(1)} %get-tuple-element.1004) | copy-start | bytes 16 | tf_op jit(solution)/shard_map/while
  701.4 19.3 %copy-start.17 = (s32[]{:T(128)}, s32[]{:T(128)S(1)}, u32[]{:S(2)}) copy-start(s32[]{:T(128)S(1)} %get-tuple-element.1003) | copy-start | bytes 16 | tf_op jit(solution)/shard_map/while
  752.3 19.3 %copy-start.17 = (s32[]{:T(128)}, s32[]{:T(128)S(1)}, u32[]{:S(2)}) copy-start(s32[]{:T(128)S(1)} %get-tuple-element.1003) | copy-start | bytes 16 | tf_op jit(solution)/shard_map/while
  803.2 19.3 %copy-start.17 = (s32[]{:T(128)}, s32[]{:T(128)S(1)}, u32[]{:S(2)}) copy-start(s32[]{:T(128)S(1)} %get-tuple-element.1003) | copy-start | bytes 16 | tf_op jit(solution)/shard_map/while
  854.1 19.3 %copy-start.17 = (s32[]{:T(128)}, s32[]{:T(128)S(1)}, u32[]{:S(2)}) copy-start(s32[]{:T(128)S(1)} %get-tuple-element.1003) | copy-start | bytes 16 | tf_op jit(solution)/shard_map/while
  905.0 19.3 %copy-start.17 = (s32[]{:T(128)}, s32[]{:T(128)S(1)}, u32[]{:S(2)}) copy-start(s32[]{:T(128)S(1)} %get-tuple-element.1003) | copy-start | bytes 16 | tf_op jit(solution)/shard_map/while
  955.9 19.3 %copy-start.17 = (s32[]{:T(128)}, s32[]{:T(128)S(1)}, u32[]{:S(2)}) copy-start(s32[]{:T(128)S(1)} %get-tuple-element.1003) | copy-start | bytes 16 | tf_op jit(solution)/shard_map/while
  (200 other events, 650.9 us)
Sparse Core Ops, SparseCore 0:
  9.0 184.2 all-gather.1
  1038.1 48.2 reduce-scatter.1
